TPU v7x, 128 devices: a whole 4x4x4 slice. The times are simulated.
128 devices in a mesh: fsdp: 8 (over x, core), owner: 16 (over y, z).
Axes of the slice: x: 4, y: 4, z: 4, core: 2. Of those that a mesh axis runs over, the one named last changes fastest.
Arguments:
- grads: bfloat16 [32, 2560, 5120], P('owner', 'fsdp'), may hold values from -6 to 6
- assign: int32 [320, 1], replicated, may hold values from 0 to 15; in each aligned block of 20 rows (0 to 19, 20 to 39, ...) at most 2 rows name the same one
- bases: bfloat16 [16, 32, 512, 512], P('owner', None, 'fsdp'), may hold values from -0.25 to 0.25
- eigvals: bfloat16 [16, 32, 512], P('owner'), may hold values from 0.099609375 to 10
Outputs:
- update: bfloat16 [32, 2560, 5120], P('owner', 'fsdp')
Inputs may be any that keep to these rules, and one draw needn't show every extreme that they name: `assign`: within each aligned block of 20 units (the matrices of one index of owner) no owner is named more than 2 times; in some block one owner is named exactly 2 times.
All inputs are finite; a program needn't handle non-finite values.
Results may differ from a plain program's by a relative error of at most 0.0043.
Values may be sent and summed in bfloat16 or wider, within the bound.
No kernel may reach another device: no remote copies, remote signals or barrier semaphores. Data moves between devices by JAX's collectives and lax.ppermute only.
A program may use at most 128 MiB of HBM per device.

v0:
```python
import jax
import jax.numpy as jnp
from jax import lax
from jax.sharding import PartitionSpec as P

BLK = 512


DAMPING = 0.1


def rotate(panel_block, basis_block, eigen_vals):
    turned = jnp.einsum(
        "srk,skc->src", panel_block, basis_block, preferred_element_type=jnp.float32
    )
    scaled = (turned / (eigen_vals.astype(jnp.float32)[:, None, :] + DAMPING)).astype(jnp.bfloat16)
    return jnp.einsum(
        "srk,sck->src", scaled, basis_block, preferred_element_type=jnp.float32
    ).astype(jnp.bfloat16)


def per_device(grads, assign, bases, eigvals):
    owner_count = lax.axis_size("owner")
    owner_here = lax.axis_index("owner")
    matrices, row_count, col_count = grads.shape
    block_count = col_count // BLK
    unit_count = matrices * block_count
    slot_count = bases.shape[1]
    per_peer = slot_count // owner_count
    owner_table = assign[:, 0].reshape(owner_count, unit_count)
    owner_ids = jnp.arange(owner_count, dtype=jnp.int32)
    owner_hits = (owner_table[:, :, None] == owner_ids[None, None, :]).astype(jnp.int32)
    slot_ranks = jnp.sum((jnp.cumsum(owner_hits, axis=1) - 1) * owner_hits, axis=2)
    my_owners = lax.dynamic_index_in_dim(owner_table, owner_here, 0, keepdims=False)
    my_rank = lax.dynamic_index_in_dim(slot_ranks, owner_here, 0, keepdims=False)
    my_slots = my_owners * per_peer + my_rank
    panels = (
        grads.reshape(matrices, row_count, block_count, BLK)
        .transpose(0, 2, 1, 3)
        .reshape(unit_count, row_count, BLK)
    )
    base_local = bases[0]
    eigen_local = eigvals[0]
    slot_match = (my_owners[:, None, None] == owner_ids[None, :, None]) & (
        my_rank[:, None, None] == jnp.arange(per_peer, dtype=jnp.int32)[None, None, :]
    )
    unit_ids = jnp.arange(unit_count, dtype=jnp.int32)[:, None, None]
    slot_index = jnp.sum(jnp.where(slot_match, unit_ids, 0), axis=0) + jnp.where(
        jnp.any(slot_match, axis=0), 0, unit_count
    )
    padded_panels = jnp.concatenate([panels, jnp.zeros((1, row_count, BLK), panels.dtype)], axis=0)
    outgoing = padded_panels[slot_index.reshape(-1)]
    incoming = lax.all_to_all(outgoing, "owner", split_axis=0, concat_axis=0, tiled=True)
    full_bases = lax.all_gather(base_local, "fsdp", axis=1, tiled=True)
    rotated_all = rotate(incoming, full_bases, eigen_local)
    returned = lax.all_to_all(rotated_all, "owner", split_axis=0, concat_axis=0, tiled=True)
    finished = returned[my_slots]
    return (
        finished.reshape(matrices, block_count, row_count, BLK)
        .transpose(0, 2, 1, 3)
        .reshape(matrices, row_count, col_count)
    )


def solution(mesh):
    in_specs = (
        P("owner", "fsdp", None),
        P(),
        P("owner", None, "fsdp", None),
        P("owner", None, None),
    )
    out_specs = P("owner", "fsdp", None)
    return jax.shard_map(
        per_device, mesh=mesh, in_specs=in_specs, out_specs=out_specs, check_vma=False
    )
```

profile of v0, /device:TPU:1, one launch (start us, length us, event | category | flops | bytes accessed | tf_op | source)
XLA Modules:
  0.0 481.3 jit_solution(13286742870900075079)
XLA Ops:
  6.5 0.0 all-gather.3.cloned.1.call-start
  6.5 0.7 all-gather.3.cloned.1.call-update
  7.3 0.7 reduce
  8.0 0.1 reshape_squeeze.3
  8.1 0.1 copy.24
  8.1 0.5 fusion.20
  8.7 0.2 add_reduce_fusion
  8.9 0.1 and_reduce_fusion
  9.0 0.1 fusion.17
  9.2 0.1 copy.26
  9.3 0.1 add.74
  9.3 9.9 %copy.22 = bf16[2,320,5120]{1,2,0:T(8,128)(2,1)} copy(bf16[2,320,5120]{2,1,0:T(8,128)(2,1)} %param.4) | data formatting | bytes 13107200 | tf_op args[0]
  19.2 10.4 %copy.23 = bf16[2,10,320,512]{3,2,1,0:T(8,128)(2,1)} copy(bf16[2,10,320,512]{2,3,1,0:T(8,128)(2,1)} %bitcast.31) | data formatting | bytes 13107200 | tf_op jit(solution)/shard_map/transpose | solution.py:39
  29.6 6.5 %concatenate.3 = bf16[21,320,512]{2,1,0:T(8,128)(2,1)} pad(bf16[20,320,512]{2,1,0:T(8,128)(2,1)} %bitcast.33, bf16[]{:T(256)} %constant.11.clone.1), padding=0_1x0_0x0_0 | pad | bytes 13434882 | tf_op jit(solution)/shard_map/concatenate | solution.py:51
  36.2 8.9 %gather_fusion = bf16[32,320,512]{2,1,0:T(8,128)(2,1)} fusion(bf16[21,320,512]{2,1,0:T(8,128)(2,1)} %concatenate.3, s32[1024]{0:T(1024)S(1)} %pad_clamp_fusion.1), kind=kCustom, calls=%fused_computation | custom fusion | bytes 20971648 | tf_op jit(solution)/shard_map/gather | solution.py:52
  45.0 9.2 %all-to-all-start = ((bf16[32,320,512]{2,1,0:T(8,128)(2,1)}), bf16[32,320,512]{2,1,0:T(8,128)(2,1)}, u32[]{:S(2)}, u32[]{:S(2)}) async-start(bf16[32,320,512]{2,1,0:T(8,128)(2,1)} %gather_fusion), calls=%async_computation | async-start | bytes 20971520 | tf_op jit(solution)/shard_map/all_to_all | solution.py:53
  54.2 0.0 copy-done
  54.3 180.6 %all-to-all-done = bf16[32,320,512]{2,1,0:T(8,128)(2,1)} async-done(((bf16[32,320,512]{2,1,0:T(8,128)(2,1)}), bf16[32,320,512]{2,1,0:T(8,128)(2,1)}, u32[]{:S(2)}, u32[]{:S(2)}) %all-to-all-start) | async-done | bytes 10485792 | tf_op jit(solution)/shard_map/all_to_all | solution.py:53
  234.9 23.9 %fusion.9 = bf16[32,320,512]{2,1,0:T(8,128)(2,1)} fusion(bf16[1,32,512,512]{3,2,1,0:T(8,128)(2,1)} %all-gather.3.cloned.1.call-done, f32[32,512]{1,0:T(8,128)S(1)} %add_bitcast_fusion, bf16[32,320,512]{2,1,0:T(8,128)(2,1)} %all-to-all-done), kind=kOutput, calls=%fused_computation.8 | convolution fusion | flops 10753146880 | bytes 37814272 | tf_op jit(solution)/shard_map/srk,sck->src/dot_general | solution.py:17
  258.8 11.8 %all-to-all-start.1 = ((bf16[32,320,512]{2,1,0:T(8,128)(2,1)}), bf16[32,320,512]{2,1,0:T(8,128)(2,1)}, u32[]{:S(2)}, u32[]{:S(2)}) async-start(bf16[32,320,512]{2,1,0:T(8,128)(2,1)} %fusion.9), calls=%async_computation.1 | async-start | bytes 20971520 | tf_op jit(solution)/shard_map/all_to_all | solution.py:56
  270.7 175.3 %all-to-all-done.1 = bf16[32,320,512]{2,1,0:T(8,128)(2,1)} async-done(((bf16[32,320,512]{2,1,0:T(8,128)(2,1)}), bf16[32,320,512]{2,1,0:T(8,128)(2,1)}, u32[]{:S(2)}, u32[]{:S(2)}) %all-to-all-start.1) | async-done | bytes 10485792 | tf_op jit(solution)/shard_map/all_to_all | solution.py:56
  446.0 8.8 %gather_fusion.1 = bf16[20,320,512]{2,1,0:T(8,128)(2,1)} fusion(bf16[32,320,512]{2,1,0:T(8,128)(2,1)} %all-to-all-done.1, s32[1024]{0:T(1024)S(1)} %pad_clamp_fusion), kind=kCustom, calls=%fused_computation.1 | custom fusion | bytes 13107280 | tf_op jit(solution)/shard_map/gather | solution.py:57
  454.8 9.8 %copy.27 = bf16[2,10,320,512]{2,3,1,0:T(8,128)(2,1)} copy(bf16[2,10,320,512]{3,2,1,0:T(8,128)(2,1)} %bitcast.32) | data formatting | bytes 13107200 | tf_op jit(solution)/shard_map/reshape | solution.py:59
  464.6 9.9 %copy.28 = bf16[2,320,5120]{2,1,0:T(8,128)(2,1)} copy(bf16[2,320,5120]{1,2,0:T(8,128)(2,1)} %bitcast.30) | data formatting | bytes 13107200 | tf_op jit(solution)/shard_map/reshape | solution.py:61
  (10 shorter events, 0.1 us)
Async XLA Ops:
  6.5 228.3 %all-gather.3.cloned.1.call-start = ((), (), s32[]{:S(2)}) async-start(), calls=%async_computation.2 | async-start | bytes 18874368 | tf_op jit(solution)/shard_map/all_gather | solution.py:54
  45.0 9.2 %copy-start = (bf16[1,32,512]{2,1,0:T(8,128)(2,1)S(1)}, bf16[1,32,512]{2,1,0:T(8,128)(2,1)}, u32[]{:S(2)}) copy-start(bf16[1,32,512]{2,1,0:T(8,128)(2,1)} %param.7) | copy-start | bytes 98308
  45.0 189.8 %all-to-all-start = ((bf16[32,320,512]{2,1,0:T(8,128)(2,1)}), bf16[32,320,512]{2,1,0:T(8,128)(2,1)}, u32[]{:S(2)}, u32[]{:S(2)}) async-start(bf16[32,320,512]{2,1,0:T(8,128)(2,1)} %gather_fusion), calls=%async_computation | async-start | bytes 20971520 | tf_op jit(solution)/shard_map/all_to_all | solution.py:53
  258.8 187.2 %all-to-all-start.1 = ((bf16[32,320,512]{2,1,0:T(8,128)(2,1)}), bf16[32,320,512]{2,1,0:T(8,128)(2,1)}, u32[]{:S(2)}, u32[]{:S(2)}) async-start(bf16[32,320,512]{2,1,0:T(8,128)(2,1)} %fusion.9), calls=%async_computation.1 | async-start | bytes 20971520 | tf_op jit(solution)/shard_map/all_to_all | solution.py:56
Sparse Core Ops, SparseCore 0:
  9.0 88.4 all-gather.2
where the time goes:
time: 487 us; the launch traced here: 481 us
  waiting for transfers between devices  357 us (73%)
  local copies, waits for them, and re-layouts  64.5 us (13%)
  matrix products  23.9 us (5%)
  starting transfers between devices  21 us (4%)
  between operations  13.5 us (3%)
    all_to_all x1, waiting for transfers between devices, per_device(): lax.all_to_all(outgoing, 'owner', split_axis=0, concat_axis=0, tiled=True)  181 us
    all_to_all x1, waiting for transfers between devices, per_device(): lax.all_to_all(rotated_all, 'owner', split_axis=0, concat_axis=0, tiled=T...  175 us
    dot_general x1, matrix products, rotate(): jnp.einsum('srk,sck->src', scaled, basis_block, preferred_element_type=jn...  23.9 us
    all_to_all x1, starting transfers between devices, per_device(): lax.all_to_all(rotated_all, 'owner', split_axis=0, concat_axis=0, tiled=T...  11.8 us
    transpose x1, local copies, waits for them, and re-layouts, per_device(): panels = grads.reshape(matrices, row_count, block_count, BLK).transpose(0...  10.4 us
    unnamed x3, local copies, waits for them, and re-layouts  9.86 us
    reshape x1, local copies, waits for them, and re-layouts, per_device(): return finished.reshape(matrices, block_count, row_count, BLK).transpose(...  9.85 us
    reshape x1, local copies, waits for them, and re-layouts, per_device(): finished.reshape(matrices, block_count, row_count, BLK)  9.84 us
  transfers between devices with their start and end apart: 3, of which 2 were waited for; matrix products, arithmetic and copies ran while one was open for 8% of the time, Pallas kernels for 0%

commit v1 on v0

v1 whole, which is shorter than its diff:
```python
import jax
import jax.numpy as jnp
from jax import lax
from jax.experimental import pallas as pl
from jax.experimental.pallas import tpu as pltpu
from jax.sharding import PartitionSpec as P

BLK = 512
DAMPING = 0.1


def rotate_kernel(grad_ref, basis_ref, eigen_ref, out_ref):
    shards, _, shard_rows, width = basis_ref.shape
    basis = basis_ref[...].reshape(shards * shard_rows, width)
    inverse = 1.0 / (eigen_ref[0].astype(jnp.float32) + DAMPING)
    turned = jnp.dot(grad_ref[0], basis, preferred_element_type=jnp.float32)
    scaled = (turned * inverse).astype(jnp.bfloat16)
    out_ref[0] = lax.dot_general(
        scaled, basis, (((1,), (1,)), ((), ())), preferred_element_type=jnp.float32
    ).astype(out_ref.dtype)


def rotate(grads, bases, eigen):
    matrices, row_count, col_count = grads.shape
    block_count = col_count // BLK
    shards, unit_count, shard_rows, width = bases.shape
    flops = 4 * unit_count * row_count * BLK * BLK
    moved = 2 * (2 * grads.size + bases.size)
    return pl.pallas_call(
        rotate_kernel,
        out_shape=jax.ShapeDtypeStruct(grads.shape, grads.dtype),
        grid=(unit_count,),
        in_specs=[
            pl.BlockSpec((1, row_count, BLK), lambda u: (u // block_count, 0, u % block_count)),
            pl.BlockSpec((shards, 1, shard_rows, width), lambda u: (0, u, 0, 0)),
            pl.BlockSpec((1, 1, BLK), lambda u: (u, 0, 0)),
        ],
        out_specs=pl.BlockSpec(
            (1, row_count, BLK), lambda u: (u // block_count, 0, u % block_count)
        ),
        cost_estimate=pl.CostEstimate(flops=flops, bytes_accessed=moved, transcendentals=0),
        name="rotate",
    )(grads, bases, eigen.reshape(unit_count, 1, BLK))


def per_device(grads, assign, bases, eigvals):
    owner_count = lax.axis_size("owner")
    owner_here = lax.axis_index("owner")
    matrices, row_count, col_count = grads.shape
    unit_count = matrices * (col_count // BLK)
    per_peer = bases.shape[1] // owner_count
    owners = lax.dynamic_slice_in_dim(assign[:, 0], owner_here * unit_count, unit_count)
    units = jnp.arange(unit_count, dtype=jnp.int32)
    same = (owners[:, None] == owners[None, :]) & (units[None, :] < units[:, None])
    slots = owners * per_peer + jnp.sum(same.astype(jnp.int32), axis=1)
    arrived = lax.all_to_all(bases[0], "owner", split_axis=0, concat_axis=0, tiled=True)
    eigen = lax.all_to_all(eigvals[0], "owner", split_axis=0, concat_axis=0, tiled=True)
    mine = arrived[slots]
    whole = lax.all_gather(mine, "fsdp", axis=0)
    return rotate(grads, whole, eigen[slots])


def solution(mesh):
    in_specs = (
        P("owner", "fsdp", None),
        P(),
        P("owner", None, "fsdp", None),
        P("owner", None, None),
    )
    out_specs = P("owner", "fsdp", None)
    return jax.shard_map(
        per_device, mesh=mesh, in_specs=in_specs, out_specs=out_specs, check_vma=False
    )
```

time: 487 us -> 132 us (0.27); the launches traced: 481 us -> 132 us
  waiting for transfers between devices: 357 us -> 76 us
  local copies, waits for them, and re-layouts: 64.5 us -> 3.13 us
  matrix products: 23.9 us -> 0 us
  Pallas kernels: 0 us -> 20.2 us
  starting transfers between devices: 21 us -> 8.76 us
  blocking collectives: 0 us -> 9.94 us
    all_to_all x2 -> x1, waiting for transfers between devices: 356 us -> 27.7 us  [per_device(): lax.all_to_all(bases[0], 'owner', split_axis=0, concat_axis=0, tiled=True)]
    all_gather x1, waiting for transfers between devices: 0.01 us -> 48.2 us  [per_device(): whole = lax.all_gather(mine, 'fsdp', axis=0)]
    dot_general x1 -> x0, matrix products: 23.9 us -> none  [rotate(): jnp.einsum('srk,sck->src', scaled, basis_block, preferred_element_type=jn...]
    pallas_call x0 -> x1, Pallas kernels: none -> 20.2 us  [rotate(): pl.pallas_call(rotate_kernel, out_shape=jax.ShapeDtypeStruct(grads.shape,...]
    reshape x2 -> x1, local copies, waits for them, and re-layouts: 19.7 us -> 0.64 us  [rotate(): eigen.reshape(unit_count, 1, BLK)]
    gather x2, local copies, waits for them, and re-layouts: 17.6 us -> 2.36 us  [the longest x1 1.76 us: per_device(): mine = arrived[slots]]
    all_to_all x2 -> x1, starting transfers between devices: 21 us -> 8.72 us  [per_device(): lax.all_to_all(bases[0], 'owner', split_axis=0, concat_axis=0, tiled=True)]
    transpose x1 -> x0, local copies, waits for them, and re-layouts: 10.4 us -> none  [per_device(): panels = grads.reshape(matrices, row_count, block_count, BLK).transpose(0...]
  transfers between devices with their start and end apart: 3 -> 2, of which waited for: 2 -> 2; matrix products, arithmetic and copies ran while one was open for 8% -> 1% of each run, Pallas kernels for 0% -> 0%
where the time goes in v1:
time: 132 us
  waiting for transfers between devices  76 us (58%)
  Pallas kernels  20.2 us (15%)
  between operations  13.4 us (10%)
  blocking collectives  9.94 us (8%)
  starting transfers between devices  8.76 us (7%)
  local copies, waits for them, and re-layouts  3.13 us (2%)
    all_gather x1, waiting for transfers between devices, per_device(): whole = lax.all_gather(mine, 'fsdp', axis=0)  48.2 us
    all_to_all x1, waiting for transfers between devices, per_device(): lax.all_to_all(bases[0], 'owner', split_axis=0, concat_axis=0, tiled=True)  27.7 us
    pallas_call x1, Pallas kernels, rotate(): pl.pallas_call(rotate_kernel, out_shape=jax.ShapeDtypeStruct(grads.shape,...  20.2 us
    all_to_all x1, blocking collectives, per_device(): lax.all_to_all(eigvals[0], 'owner', split_axis=0, concat_axis=0, tiled=True)  9.94 us
    all_to_all x1, starting transfers between devices, per_device(): lax.all_to_all(bases[0], 'owner', split_axis=0, concat_axis=0, tiled=True)  8.72 us
  transfers between devices with their start and end apart: 2, of which 2 were waited for; matrix products, arithmetic and copies ran while one was open for 1% of the time, Pallas kernels for 0%

profile of v1, /device:TPU:1, one launch (start us, length us, event | category | flops | bytes accessed | tf_op | source)
XLA Modules:
  0.0 131.7 jit_solution(2229321382922750855)
XLA Ops:
  6.5 0.0 copy-start.1
  6.5 8.7 %all-to-all-start = ((bf16[32,64,512]{2,1,0:T(8,128)(2,1)}), bf16[32,64,512]{2,1,0:T(8,128)(2,1)S(1)}, u32[]{:S(2)}, u32[]{:S(2)}) async-start(bf16[32,64,512]{2,1,0:T(8,128)(2,1)} %bitcast.11), calls=%async_computation | async-start | bytes 4194304 | tf_op jit(solution)/shard_map/all_to_all | solution.py:56
  15.3 0.0 copy-start
  15.3 0.0 all-gather.3.cloned.1.call-start
  15.3 0.0 copy-done.1
  15.3 0.1 fusion.2
  15.4 0.2 convert_reduce_fusion
  15.6 0.1 fusion.1
  15.7 27.7 %all-to-all-done = bf16[32,64,512]{2,1,0:T(8,128)(2,1)S(1)} async-done(((bf16[32,64,512]{2,1,0:T(8,128)(2,1)}), bf16[32,64,512]{2,1,0:T(8,128)(2,1)S(1)}, u32[]{:S(2)}, u32[]{:S(2)}) %all-to-all-start) | async-done | bytes 2097184 | tf_op jit(solution)/shard_map/all_to_all | solution.py:56
  43.4 1.8 %gather_fusion = bf16[20,64,512]{2,1,0:T(8,128)(2,1)} fusion(bf16[32,64,512]{2,1,0:T(8,128)(2,1)S(1)} %all-to-all-done, s32[1024]{0:T(1024)S(1)} %pad_clamp_fusion), kind=kCustom, calls=%fused_computation | custom fusion | bytes 2621520 | tf_op jit(solution)/shard_map/gather | solution.py:58
  45.2 0.0 all-gather.3.cloned.1.call-update
  45.2 0.0 copy-done
  45.2 9.9 %all_to_all.17 = bf16[16,2,512]{2,1,0:T(2,128)(2,1)S(1)} all-to-all(bf16[16,2,512]{2,1,0:T(2,128)(2,1)S(1)} %all_to_all.12), channel_id=1, replica_groups=mesh['fsdp'=8,'owner'=16] {'owner'}, dimensions={0} | all-to-all | bytes 65536 | tf_op jit(solution)/shard_map/all_to_all | solution.py:57
  55.2 0.6 gather_fusion.1
  55.8 0.6 copy.7.eigen_ref
  56.4 48.2 %all-gather.3.cloned.1.call-done = bf16[160,64,512]{2,1,0:T(8,128)(2,1)} async-done(((bf16[20,64,512]{2,1,0:T(8,128)(2,1)}), bf16[160,64,512]{2,1,0:T(8,128)(2,1)}) %all-gather.3.cloned.1.call-update) | async-done | bytes 10485776 | tf_op jit(solution)/shard_map/all_gather | solution.py:59
  104.6 20.2 %rotate.1 = bf16[2,320,5120]{2,1,0:T(8,128)(2,1)} custom-call(bf16[2,320,5120]{2,1,0:T(8,128)(2,1)} %grad_ref.1, bf16[8,20,64,512]{3,2,1,0:T(8,128)(2,1)} %bitcast.13, bf16[20,1,512]{2,1,0:T(2,128)(2,1)} %copy.7.eigen_ref), custom_call_target="tpu_custom_call" | custom-call | flops 6710886400 | bytes 23592960 | tf_op jit(solution)/shard_map/rotate/pallas_call | solution.py:29
  (3 shorter events, 0.0 us)
Async XLA Ops:
  6.5 8.8 %copy-start.1 = (s32[320,1]{0,1:T(1,128)S(1)}, s32[320,1]{0,1:T(1,128)}, u32[]{:S(2)}) copy-start(s32[320,1]{0,1:T(1,128)} %param.5) | copy-start | bytes 3844
  6.5 36.9 %all-to-all-start = ((bf16[32,64,512]{2,1,0:T(8,128)(2,1)}), bf16[32,64,512]{2,1,0:T(8,128)(2,1)S(1)}, u32[]{:S(2)}, u32[]{:S(2)}) async-start(bf16[32,64,512]{2,1,0:T(8,128)(2,1)} %bitcast.11), calls=%async_computation | async-start | bytes 4194304 | tf_op jit(solution)/shard_map/all_to_all | solution.py:56
  15.3 30.0 %copy-start = (bf16[1,32,512]{2,1,0:T(8,128)(2,1)S(1)}, bf16[1,32,512]{2,1,0:T(8,128)(2,1)}, u32[]{:S(2)}) copy-start(bf16[1,32,512]{2,1,0:T(8,128)(2,1)} %param.7) | copy-start | bytes 98308
  15.3 89.4 %all-gather.3.cloned.1.call-start = ((), (), s32[]{:S(2)}) async-start(), calls=%async_computation.2 | async-start | bytes 11796480 | tf_op jit(solution)/shard_map/all_gather | solution.py:59
Sparse Core Ops, SparseCore 0:
  45.3 59.2 all-gather.2
